TPU v7x, 128 devices: a whole 4x4x4 slice. The times are simulated.
128 devices in a mesh: dp: 16 (over x, y), expert: 8 (over z, core).
Axes of the slice: x: 4, y: 4, z: 4, core: 2. Of those that a mesh axis runs over, the one named last changes fastest.
Arguments:
- tokens: bfloat16 [2048, 4096], P('dp', 'expert'), may hold values from -6 to 6
- output_gradient: bfloat16 [2048, 4096], P('dp', 'expert'), may hold values from -6 to 6
- routing: int32 [2048, 2], P('dp'), may hold values from 0 to 7, all different within a row; in each aligned block of 128 rows (0 to 127, 128 to 255, ...) at most 96 rows name the same one
- router_gate_values: float32 [2048, 2], P('dp'), may hold values from 0.1 to 0.9
- gate_weight: bfloat16 [8, 7168, 4096], P('expert', 'dp'), may hold values from -0.09375 to 0.09375
- up_weight: bfloat16 [8, 7168, 4096], P('expert', 'dp'), may hold values from -0.09375 to 0.09375
- down_weight: bfloat16 [8, 7168, 4096], P('expert', 'dp'), may hold values from -0.0625 to 0.0625
- adapter_lower_gate: bfloat16 [8, 16, 4096], P('expert'), may hold values from -0.09375 to 0.09375
- adapter_upper_gate: bfloat16 [8, 7168, 16], P('expert', 'dp'), may hold values from -0.375 to 0.375
- adapter_lower_up: bfloat16 [8, 16, 4096], P('expert'), may hold values from -0.09375 to 0.09375
- adapter_upper_up: bfloat16 [8, 7168, 16], P('expert', 'dp'), may hold values from -0.375 to 0.375
- adapter_lower_down: bfloat16 [8, 16, 7168], P('expert', None, 'dp'), may hold values from -0.0625 to 0.0625
- adapter_upper_down: bfloat16 [8, 4096, 16], P('expert'), may hold values from -0.375 to 0.375
Outputs:
- grad_x: bfloat16 [2048, 4096], P('dp', 'expert')
- grad_lora_a_gate: float32 [8, 16, 4096], P('expert')
- grad_lora_b_gate: float32 [8, 7168, 16], P('expert', 'dp')
- grad_lora_a_up: float32 [8, 16, 4096], P('expert')
- grad_lora_b_up: float32 [8, 7168, 16], P('expert', 'dp')
- grad_lora_a_down: float32 [8, 16, 7168], P('expert', None, 'dp')
- grad_lora_b_down: float32 [8, 4096, 16], P('expert')
Inputs may be any that keep to these rules, and one draw needn't show every extreme that they name: `routing`: each row names two different experts. In the rows of one dp shard (aligned blocks of 128 rows) no expert is named by more than 96 rows, and in some blocks one expert is named by exactly 96 rows.
All inputs are finite; a program needn't handle non-finite values.
Results may differ from a plain program's by a relative error of at most 0.015.
Values may be sent and summed in bfloat16 or wider, within the bound.
A program may use at most 256 MiB of HBM per device.

v0:
```python
import jax
import jax.numpy as jnp
from jax import lax
from jax.sharding import PartitionSpec as P

ADAPTER_SCALE = 2.0
NUM_CHUNKS = 2


def contract_pair(left, right, left_axis, right_axis):
    return lax.dot_general(
        left, right, (((left_axis,), (right_axis,)), ((), ())), preferred_element_type=jnp.float32
    )


def slot_numbers(route_rows, experts):
    picked = (route_rows[:, :, None] == jnp.arange(experts, dtype=jnp.int32)[None, None, :]).astype(
        jnp.int32
    )
    per_token = jnp.sum(picked, axis=1)
    earlier = jnp.cumsum(per_token, axis=0) - per_token
    return jnp.sum(earlier[:, None, :] * picked, axis=2)


def slot_sources(route_rows, positions, experts, capacity):
    tokens_here, choose = route_rows.shape
    target = (route_rows * capacity + positions).reshape(-1)
    owners = jnp.repeat(jnp.arange(tokens_here, dtype=jnp.int32), choose)
    member_ids = jnp.tile(jnp.arange(choose, dtype=jnp.int32), tokens_here)
    source = jnp.full((experts * capacity,), tokens_here, jnp.int32).at[target].set(owners)
    member = jnp.zeros((experts * capacity,), jnp.int32).at[target].set(member_ids)
    return (source, member)


def rows_backward_pass(input_rows, output_gradient_rows, params):
    (
        gate_weight,
        up_weight,
        down_weight,
        a_gate,
        gate_adapter_upper,
        a_up,
        up_adapter_upper,
        down_adapter_lower,
        b_down,
    ) = params
    gate_projected_lower = contract_pair(a_gate, input_rows, 1, 1).astype(jnp.bfloat16)
    up_projected_lower = contract_pair(a_up, input_rows, 1, 1).astype(jnp.bfloat16)
    gate_preactivation = contract_pair(
        gate_weight, input_rows, 1, 1
    ) + ADAPTER_SCALE * contract_pair(gate_adapter_upper, gate_projected_lower, 1, 0)
    up_preactivation = contract_pair(up_weight, input_rows, 1, 1) + ADAPTER_SCALE * contract_pair(
        up_adapter_upper, up_projected_lower, 1, 0
    )
    sigmoid_gate = jax.nn.sigmoid(gate_preactivation)
    silu_gate = gate_preactivation * sigmoid_gate
    hidden_units = (silu_gate * up_preactivation).astype(jnp.bfloat16)
    down_projected_lower = contract_pair(b_down, output_gradient_rows, 0, 1).astype(jnp.bfloat16)
    hidden_gradient = contract_pair(
        down_weight, output_gradient_rows, 1, 1
    ) + ADAPTER_SCALE * contract_pair(down_adapter_lower, down_projected_lower, 0, 0)
    gate_gradient = (
        hidden_gradient
        * up_preactivation
        * sigmoid_gate
        * (1.0 + gate_preactivation * (1.0 - sigmoid_gate))
    ).astype(jnp.bfloat16)
    up_gradient = (hidden_gradient * silu_gate).astype(jnp.bfloat16)
    gate_partial = contract_pair(gate_adapter_upper, gate_gradient, 0, 0).astype(jnp.bfloat16)
    up_partial = contract_pair(up_adapter_upper, up_gradient, 0, 0).astype(jnp.bfloat16)
    down_partial = contract_pair(down_adapter_lower, hidden_units, 1, 0).astype(jnp.bfloat16)
    paired_partials = jnp.concatenate([gate_partial, up_partial], 0)
    paired_factors = jnp.concatenate([a_gate, a_up], 0)
    gradient_rows_out = (
        contract_pair(gate_gradient, gate_weight, 0, 0)
        + contract_pair(up_gradient, up_weight, 0, 0)
        + ADAPTER_SCALE * contract_pair(paired_partials, paired_factors, 0, 0)
    )
    shared_slice = (
        ADAPTER_SCALE * contract_pair(gate_partial, input_rows, 1, 0),
        ADAPTER_SCALE * contract_pair(up_partial, input_rows, 1, 0),
        ADAPTER_SCALE * contract_pair(output_gradient_rows, down_partial, 0, 1),
    )
    owned_slice = (
        ADAPTER_SCALE * contract_pair(gate_gradient, gate_projected_lower, 1, 1),
        ADAPTER_SCALE * contract_pair(up_gradient, up_projected_lower, 1, 1),
        ADAPTER_SCALE * contract_pair(down_projected_lower, hidden_units, 1, 1),
    )
    return (gradient_rows_out, shared_slice, owned_slice)


def local(
    tokens,
    output_gradient,
    routing,
    router_gate_values,
    gate_weight,
    up_weight,
    down_weight,
    adapter_lower_gate,
    adapter_upper_gate,
    adapter_lower_up,
    adapter_upper_up,
    adapter_lower_down,
    adapter_upper_down,
):
    experts = lax.axis_size("expert")
    shards = lax.axis_size("dp")
    tok_local, feat_local = tokens.shape
    choose = routing.shape[1]
    complete_width = feat_local * experts
    capacity = min(tok_local, 6 * tok_local // experts)
    adapter_rank = adapter_lower_gate.shape[1]
    chunks = NUM_CHUNKS
    piece = capacity // chunks
    params = (
        gate_weight[0],
        up_weight[0],
        down_weight[0],
        adapter_lower_gate[0],
        adapter_upper_gate[0],
        adapter_lower_up[0],
        adapter_upper_up[0],
        adapter_lower_down[0],
        adapter_upper_down[0],
    )
    positions = slot_numbers(routing, experts)
    zero_row = jnp.zeros((1, feat_local), jnp.bfloat16)
    source, member = slot_sources(routing, positions, experts, capacity)
    clamped = jnp.minimum(source, tok_local - 1)
    slot_gate = jnp.where(
        source < tok_local, router_gate_values.reshape(-1)[clamped * choose + member], 0.0
    )
    send_x = jnp.concatenate([tokens, zero_row], 0)[source].reshape(experts, capacity, feat_local)
    send_dy = (
        (
            slot_gate[:, None]
            * jnp.concatenate([output_gradient, zero_row], 0)[source].astype(jnp.float32)
        )
        .astype(jnp.bfloat16)
        .reshape(experts, capacity, feat_local)
    )
    send_both = jnp.concatenate([send_x, send_dy], axis=2)
    recv_both = lax.all_to_all(send_both, "expert", split_axis=0, concat_axis=2, tiled=True)[0]
    recv_both = recv_both.reshape(capacity, experts, 2, feat_local).transpose(0, 2, 1, 3)
    recv_both = recv_both.reshape(capacity, 2 * complete_width)
    rows_pieces = []
    shared_total = None
    owned_total = None
    for c in range(chunks):
        part = recv_both[c * piece : (c + 1) * piece]
        gathered = lax.all_gather(part, "dp", axis=0, tiled=True)
        x_rows = gathered[:, :complete_width]
        dy_rows = gathered[:, complete_width:]
        rows_out, shared_slice, owned_slice = rows_backward_pass(x_rows, dy_rows, params)
        if c == 0:
            shared_total, owned_total = (shared_slice, owned_slice)
        else:
            shared_total = jax.tree.map(jnp.add, shared_total, shared_slice)
            owned_total = jax.tree.map(jnp.add, owned_total, owned_slice)
        rows_bf = rows_out.astype(jnp.bfloat16).reshape(shards, piece, complete_width)
        summed = lax.psum_scatter(rows_bf, "dp", scatter_dimension=0, tiled=True)[0]
        rows_pieces.append(summed)
    lora = jnp.concatenate([shared_total[0], shared_total[1], shared_total[2].T], 0).astype(
        jnp.bfloat16
    )
    lora_shape = lora.shape
    lora_part = lax.psum_scatter(
        lora.reshape(shards * 8, -1), "dp", scatter_dimension=0, tiled=True
    )
    summed = jnp.concatenate(rows_pieces, 0)
    lora_part = lax.optimization_barrier(lora_part)
    lora_sum = lax.all_gather(lora_part, "dp", axis=0, tiled=True).astype(jnp.float32)
    lora_sum = lora_sum.reshape(lora_shape)
    grad_a_gate = lora_sum[:adapter_rank]
    grad_a_up = lora_sum[adapter_rank : 2 * adapter_rank]
    grad_b_down = lora_sum[2 * adapter_rank :].T
    returned_rows = lax.all_to_all(
        summed.reshape(capacity, experts, feat_local),
        "expert",
        split_axis=1,
        concat_axis=1,
        tiled=True,
    ).astype(jnp.float32)
    lookup = positions * experts + routing
    grad_x = jnp.sum(returned_rows.reshape(capacity * experts, feat_local)[lookup], axis=1).astype(
        jnp.bfloat16
    )
    return (
        grad_x,
        grad_a_gate[None],
        owned_total[0][None],
        grad_a_up[None],
        owned_total[1][None],
        owned_total[2][None],
        grad_b_down[None],
    )


def solution(mesh):
    return jax.shard_map(
        local,
        mesh=mesh,
        in_specs=(
            P("dp", "expert"),
            P("dp", "expert"),
            P("dp", None),
            P("dp", None),
            P("expert", "dp", None),
            P("expert", "dp", None),
            P("expert", "dp", None),
            P("expert", None, None),
            P("expert", "dp", None),
            P("expert", None, None),
            P("expert", "dp", None),
            P("expert", None, "dp"),
            P("expert", None, None),
        ),
        out_specs=(
            P("dp", "expert"),
            P("expert", None, None),
            P("expert", "dp", None),
            P("expert", None, None),
            P("expert", "dp", None),
            P("expert", None, "dp"),
            P("expert", None, None),
        ),
        check_vma=False,
    )
```

profile of v0, /device:TPU:1, one launch (start us, length us, event | category | flops | bytes accessed | tf_op | source)
XLA Modules:
  0.0 568.4 jit_solution(9020184322485059997)
XLA Ops:
  14.7 5.0 gather_fusion.1
  19.8 2.7 gather_fusion.2
  22.5 2.7 gather_fusion
  25.7 27.4 %all_to_all.20 = bf16[8,96,1024]{2,1,0:T(8,128)(2,1)S(1)} all-to-all(bf16[8,96,1024]{2,1,0:T(8,128)(2,1)S(1)} %pad_maximum_fusion), channel_id=1, replica_groups=mesh['dp'=16,'expert'=8] {'expert'}, dimensions={0} | all-to-all | bytes 3145728 | tf_op jit(solution)/shard_map/all_to_all | solution.py:144
  60.7 88.0 %all-gather.3.cloned.1.call-done = bf16[768,8192]{1,0:T(8,128)(2,1)} async-done(((bf16[48,8192]{1,0:T(8,128)(2,1)}), bf16[768,8192]{1,0:T(8,128)(2,1)}) %all-gather.3.cloned.1.call-update) | async-done | bytes 12582928 | tf_op jit(solution)/shard_map/all_gather | solution.py:152
  148.7 4.7 fusion.79
  153.4 6.0 %fusion.31 = f32[768,448]{0,1:T(8,128)S(1)} fusion(bf16[1,448,4096]{2,1,0:T(8,128)(2,1)S(1)} %copy-done.2, bf16[768,8192]{1,0:T(8,128)(2,1)} %all-gather.3.cloned.1.call-done), kind=kOutput, calls=%fused_computation.35 | convolution fusion | flops 2818572288 | bytes 11337728 | tf_op jit(solution)/shard_map/dot_general | solution.py:11
  162.3 3.1 fusion.10
  167.9 14.7 %fusion.39 = f32[768,448]{0,1:T(8,128)S(1)} fusion(bf16[1,448,4096]{2,1,0:T(8,128)(2,1)S(1)} %copy-done.4, bf16[768,8192]{1,0:T(8,128)(2,1)S(1)} %bitcast.166), kind=kOutput, calls=%fused_computation.43 | convolution fusion | flops 2818572288 | bytes 11337728 | tf_op jit(solution)/shard_map/dot_general | solution.py:11
  184.8 6.6 %fusion.29 = f32[768,4096]{1,0:T(8,128)} fusion(bf16[448,768]{1,0:T(8,128)(2,1)S(1)} %get-tuple-element.8, bf16[1,448,4096]{2,1,0:T(8,128)(2,1)S(1)} %copy-done.2), kind=kOutput, calls=%fused_computation.33 | convolution fusion | flops 2818572288 | bytes 16941056 | tf_op jit(solution)/shard_map/dot_general | solution.py:11
  191.4 6.5 %fusion.37 = f32[768,4096]{1,0:T(8,128)} fusion(bf16[448,768]{1,0:T(8,128)(2,1)S(1)} %get-tuple-element.9, bf16[1,448,4096]{2,1,0:T(8,128)(2,1)S(1)} %copy-done.4), kind=kOutput, calls=%fused_computation.41 | convolution fusion | flops 2818572288 | bytes 16941056 | tf_op jit(solution)/shard_map/dot_general | solution.py:11
  197.9 42.7 %all-gather.5.cloned.1.call-done = bf16[768,8192]{1,0:T(8,128)(2,1)} async-done(((bf16[48,8192]{1,0:T(8,128)(2,1)}), bf16[768,8192]{1,0:T(8,128)(2,1)}) %all-gather.5.cloned.1.call-update) | async-done | bytes 12582928 | tf_op jit(solution)/shard_map/all_gather | solution.py:152
  240.5 4.7 fusion.91
  245.2 6.0 %fusion.4 = f32[768,448]{0,1:T(8,128)S(1)} fusion(bf16[768,8192]{1,0:T(8,128)(2,1)} %all-gather.5.cloned.1.call-done, bf16[1,448,4096]{2,1,0:T(8,128)(2,1)S(1)} %copy-done.35), kind=kOutput, calls=%fused_computation.12 | convolution fusion | flops 2818572288 | bytes 11337728 | tf_op jit(solution)/shard_map/dot_general | solution.py:11
  253.7 3.1 fusion.27
  259.2 3.3 fusion.35
  262.5 1.8 multiply_convert_fusion
  267.6 4.1 fusion
  271.7 4.4 fusion.23
  276.0 4.4 fusion.24
  280.4 4.1 fusion.20
  286.9 12.2 %add_convert_fusion.1 = bf16[768,4096]{1,0:T(8,128)(2,1)} fusion(f32[768,4096]{1,0:T(8,128)} %fusion.29, f32[768,4096]{1,0:T(8,128)} %fusion.37, bf16[16,4096]{1,0:T(8,128)(2,1)S(1)} %bitcast.186, bf16[16,4096]{1,0:T(8,128)(2,1)S(1)} %bitcast.184, bf16[16,768]{1,0:T(8,128)(2,1)} %bitcast.191, bf16[16,768]{1,0:T(8,128)(2,1)} %bitcast.190), kind=kOutput, calls=%fused_computation.7 | convolution fusion | flops 214532096 | bytes 31768576 | tf_op jit(solution)/shard_map/dot_general | solution.py:11
  299.2 8.9 %fusion.25 = f32[768,4096]{1,0:T(8,128)} fusion(bf16[448,768]{1,0:T(8,128)(2,1)S(1)} %get-tuple-element.11, bf16[1,448,4096]{2,1,0:T(8,128)(2,1)} %param.17), kind=kOutput, calls=%fused_computation.29 | convolution fusion | flops 2818572288 | bytes 16941056 | tf_op jit(solution)/shard_map/dot_general | solution.py:11
  308.1 6.4 %fusion.33 = f32[768,4096]{1,0:T(8,128)} fusion(bf16[448,768]{1,0:T(8,128)(2,1)S(1)} %get-tuple-element.12, bf16[1,448,4096]{2,1,0:T(8,128)(2,1)S(1)} %copy-done.6), kind=kOutput, calls=%fused_computation.37 | convolution fusion | flops 2818572288 | bytes 16941056 | tf_op jit(solution)/shard_map/dot_general | solution.py:11
  314.5 12.1 %add_convert_fusion = bf16[768,4096]{1,0:T(8,128)(2,1)} fusion(f32[768,4096]{1,0:T(8,128)} %fusion.25, f32[768,4096]{1,0:T(8,128)} %fusion.33, bf16[16,4096]{1,0:T(8,128)(2,1)S(1)} %bitcast.187, bf16[16,4096]{1,0:T(8,128)(2,1)S(1)} %bitcast.185, bf16[16,768]{1,0:T(8,128)(2,1)S(1)} %bitcast.193, bf16[16,768]{1,0:T(8,128)(2,1)S(1)} %bitcast.192), kind=kOutput, calls=%fused_computation.6 | convolution fusion | flops 214532096 | bytes 31768576 | tf_op jit(solution)/shard_map/dot_general | solution.py:11
  330.2 2.1 fusion.95
  334.8 34.6 %all-reduce.7.cloned.1.call-done = bf16[128,1536]{1,0:T(8,128)(2,1)} async-done(((bf16[128,1536]{1,0:T(8,128)(2,1)}), bf16[128,1536]{1,0:T(8,128)(2,1)}) %all-reduce.7.cloned.1.call-update) | async-done | bytes 393232
  370.1 18.3 %all_gather.11 = bf16[128,1536]{1,0:T(8,128)(2,1)S(1)} all-gather(bf16[8,1536]{1,0:T(8,128)(2,1)S(1)} %constant_dynamic-slice_fusion), channel_id=1, replica_groups=mesh['dp'=16,'expert'=8] {'dp'}, dimensions={0}, use_global_device_ids=true | all-gather | bytes 417792 | tf_op jit(solution)/shard_map/all_gather | solution.py:173
  388.9 65.0 %reduce-scatter.7.cloned.1.call-done = bf16[1,48,4096]{2,1,0:T(8,128)(2,1)} async-done(((bf16[16,48,4096]{2,1,0:T(8,128)(2,1)}), bf16[1,48,4096]{2,1,0:T(8,128)(2,1)}) %reduce-scatter.7.cloned.1.call-update) | async-done | bytes 393232
  455.1 82.5 %reduce-scatter.9.cloned.1.call-done = bf16[1,48,4096]{2,1,0:T(8,128)(2,1)} async-done(((bf16[16,48,4096]{2,1,0:T(8,128)(2,1)}), bf16[1,48,4096]{2,1,0:T(8,128)(2,1)}) %reduce-scatter.9.cloned.1.call-update) | async-done | bytes 393232
  539.9 6.2 %all-to-all-start.1 = ((bf16[96,8,512]{2,0,1:T(8,128)(2,1)}), bf16[96,8,512]{2,0,1:T(8,128)(2,1)S(1)}, u32[]{:S(2)}, u32[]{:S(2)}) async-start(bf16[96,8,512]{2,0,1:T(8,128)(2,1)} %pad_maximum_fusion.1), calls=%async_computation.1 | async-start | bytes 1572864 | tf_op jit(solution)/shard_map/all_to_all | solution.py:178
  547.0 11.4 %all-to-all-done.1 = bf16[96,8,512]{2,0,1:T(8,128)(2,1)S(1)} async-done(((bf16[96,8,512]{2,0,1:T(8,128)(2,1)}), bf16[96,8,512]{2,0,1:T(8,128)(2,1)S(1)}, u32[]{:S(2)}, u32[]{:S(2)}) %all-to-all-start.1) | async-done | bytes 786464 | tf_op jit(solution)/shard_map/all_to_all | solution.py:178
  (176 shorter events, 47.4 us)
Async XLA Ops:
  7.2 152.7 %copy-start = (bf16[1,4096,16]{1,2,0:T(8,128)(2,1)S(1)}, bf16[1,4096,16]{1,2,0:T(8,128)(2,1)}, u32[]{:S(2)}) copy-start(bf16[1,4096,16]{1,2,0:T(8,128)(2,1)} %param.25) | copy-start | bytes 393220
  7.2 12.6 %copy-start.18 = (bf16[128,512]{1,0:T(8,128)(2,1)S(1)}, bf16[128,512]{1,0:T(8,128)(2,1)}, u32[]{:S(2)}) copy-start(bf16[128,512]{1,0:T(8,128)(2,1)} %param.14) | copy-start | bytes 393220
  7.2 12.6 %copy-start.19 = (bf16[128,512]{1,0:T(8,128)(2,1)S(1)}, bf16[128,512]{1,0:T(8,128)(2,1)}, u32[]{:S(2)}) copy-start(bf16[128,512]{1,0:T(8,128)(2,1)} %param.13) | copy-start | bytes 393220
  7.2 141.5 %all-gather.3.cloned.1.call-start = ((), (), s32[]{:S(2)}) async-start(), calls=%async_computation.4 | async-start | bytes 13369344 | tf_op jit(solution)/shard_map/all_gather | solution.py:152
  57.3 91.4 %copy-start.7 = (bf16[1,16,4096]{2,1,0:T(8,128)(2,1)S(1)}, bf16[1,16,4096]{2,1,0:T(8,128)(2,1)}, u32[]{:S(2)}) copy-start(bf16[1,16,4096]{2,1,0:T(8,128)(2,1)} %param.20) | copy-start | bytes 393220
  58.8 181.7 %all-gather.5.cloned.1.call-start = ((), (), s32[]{:S(2)}) async-start(), calls=%async_computation.5 | async-start | bytes 13369344 | tf_op jit(solution)/shard_map/all_gather | solution.py:152
  60.4 309.0 %all-reduce.7.cloned.1.call-start = ((), (), s32[]{:S(2)}) async-start(), calls=%async_computation.6 | async-start | bytes 786432
  148.7 11.1 %slice-start = ((s8[12582912]{0:T(1024)(128)(4,1)}), s8[4194304]{0:T(1024)(128)(4,1)S(1)}, s32[]{:S(2)}) async-start(s8[12582912]{0:T(1024)(128)(4,1)} %bitcast.165), calls=%async_computation.9 | async-start | bytes 8388608
  153.4 6.0 %copy-start.20 = (bf16[768,16]{0,1:T(8,128)(2,1)}, bf16[768,16]{0,1:T(8,128)(2,1)S(1)}, u32[]{:S(2)}) copy-start(bf16[768,16]{0,1:T(8,128)(2,1)S(1)} %fusion.79) | copy-start | bytes 73732
  153.4 6.0 %copy-start.11 = (bf16[1,448,16]{1,2,0:T(8,128)(2,1)S(1)}, bf16[1,448,16]{1,2,0:T(8,128)(2,1)}, u32[]{:S(2)}) copy-start(bf16[1,448,16]{1,2,0:T(8,128)(2,1)} %param.21) | copy-start | bytes 43012
  153.4 6.4 %slice-start.1 = ((s8[12582912]{0:T(1024)(128)(4,1)}), s8[4194304]{0:T(1024)(128)(4,1)S(1)}, s32[]{:S(2)}) async-start(s8[12582912]{0:T(1024)(128)(4,1)} %bitcast.165), calls=%async_computation.10 | async-start | bytes 8388608
  153.4 6.4 %slice-start.2 = ((s8[12582912]{0:T(1024)(128)(4,1)}), s8[4194304]{0:T(1024)(128)(4,1)S(1)}, s32[]{:S(2)}) async-start(s8[12582912]{0:T(1024)(128)(4,1)} %bitcast.165), calls=%async_computation.11 | async-start | bytes 8388608
  167.9 14.7 %copy-start.29 = (bf16[768,16]{0,1:T(8,128)(2,1)}, bf16[768,16]{0,1:T(8,128)(2,1)S(1)}, u32[]{:S(2)}) copy-start(bf16[768,16]{0,1:T(8,128)(2,1)S(1)} %fusion.76) | copy-start | bytes 73732
  167.9 14.7 %copy-start.28 = (bf16[1,448,16]{1,2,0:T(8,128)(2,1)S(1)}, bf16[1,448,16]{1,2,0:T(8,128)(2,1)}, u32[]{:S(2)}) copy-start(bf16[1,448,16]{1,2,0:T(8,128)(2,1)} %param.23) | copy-start | bytes 43012
  184.6 80.2 %copy-start.12 = (bf16[768,16]{0,1:T(8,128)(2,1)}, bf16[768,16]{0,1:T(8,128)(2,1)S(1)}, u32[]{:S(2)}) copy-start(bf16[768,16]{0,1:T(8,128)(2,1)S(1)} %convolution_convert_fusion.5) | copy-start | bytes 73732
  184.8 81.9 %copy-start.13 = (bf16[768,16]{0,1:T(8,128)(2,1)}, bf16[768,16]{0,1:T(8,128)(2,1)S(1)}, u32[]{:S(2)}) copy-start(bf16[768,16]{0,1:T(8,128)(2,1)S(1)} %convolution_convert_fusion.4) | copy-start | bytes 73732
  240.5 11.1 %slice-start.6 = ((s8[12582912]{0:T(1024)(128)(4,1)}), s8[4194304]{0:T(1024)(128)(4,1)S(1)}, s32[]{:S(2)}) async-start(s8[12582912]{0:T(1024)(128)(4,1)} %bitcast.169), calls=%async_computation.15 | async-start | bytes 8388608
  245.2 6.0 %copy-start.26 = (bf16[768,16]{0,1:T(8,128)(2,1)}, bf16[768,16]{0,1:T(8,128)(2,1)S(1)}, u32[]{:S(2)}) copy-start(bf16[768,16]{0,1:T(8,128)(2,1)S(1)} %fusion.91) | copy-start | bytes 73732
  245.2 6.4 %slice-start.7 = ((s8[12582912]{0:T(1024)(128)(4,1)}), s8[4194304]{0:T(1024)(128)(4,1)S(1)}, s32[]{:S(2)}) async-start(s8[12582912]{0:T(1024)(128)(4,1)} %bitcast.169), calls=%async_computation.16 | async-start | bytes 8388608
  245.2 6.4 %slice-start.8 = ((s8[12582912]{0:T(1024)(128)(4,1)}), s8[4194304]{0:T(1024)(128)(4,1)S(1)}, s32[]{:S(2)}) async-start(s8[12582912]{0:T(1024)(128)(4,1)} %bitcast.169), calls=%async_computation.17 | async-start | bytes 8388608
  264.5 7.1 %copy-start.14 = (bf16[768,16]{0,1:T(8,128)(2,1)}, bf16[768,16]{0,1:T(8,128)(2,1)S(1)}, u32[]{:S(2)}) copy-start(bf16[768,16]{0,1:T(8,128)(2,1)S(1)} %convolution_convert_fusion.3) | copy-start | bytes 73732
  265.0 11.1 %copy-start.16 = (bf16[768,16]{0,1:T(8,128)(2,1)}, bf16[768,16]{0,1:T(8,128)(2,1)S(1)}, u32[]{:S(2)}) copy-start(bf16[768,16]{0,1:T(8,128)(2,1)S(1)} %convolution_convert_fusion.2) | copy-start | bytes 73732
  280.4 6.4 %copy-start.9 = (bf16[1,16,4096]{2,1,0:T(8,128)(2,1)S(1)}, bf16[1,16,4096]{2,1,0:T(8,128)(2,1)}, u32[]{:S(2)}) copy-start(bf16[1,16,4096]{2,1,0:T(8,128)(2,1)} %param.22) | copy-start | bytes 393220
  286.8 167.1 %reduce-scatter.7.cloned.1.call-start = ((), (), s32[]{:S(2)}) async-start(), calls=%async_computation.7 | async-start | bytes 6684672
  299.1 238.5 %reduce-scatter.9.cloned.1.call-start = ((), (), s32[]{:S(2)}) async-start(), calls=%async_computation.8 | async-start | bytes 6684672
  299.2 8.9 %copy-start.6 = (bf16[1,448,4096]{2,1,0:T(8,128)(2,1)S(1)}, bf16[1,448,4096]{2,1,0:T(8,128)(2,1)}, u32[]{:S(2)}) copy-start(bf16[1,448,4096]{2,1,0:T(8,128)(2,1)} %param.18) | copy-start | bytes 11010052
  308.1 6.4 %copy-start.15 = (bf16[768,16]{0,1:T(8,128)(2,1)S(1)}, bf16[768,16]{0,1:T(8,128)(2,1)}, u32[]{:S(2)}) copy-start(bf16[768,16]{0,1:T(8,128)(2,1)} %copy-done.14) | copy-start | bytes 73732
  308.1 6.4 %copy-start.17 = (bf16[768,16]{0,1:T(8,128)(2,1)S(1)}, bf16[768,16]{0,1:T(8,128)(2,1)}, u32[]{:S(2)}) copy-start(bf16[768,16]{0,1:T(8,128)(2,1)} %copy-done.16) | copy-start | bytes 73732
  326.7 5.9 %copy-start.32 = (bf16[768,16]{0,1:T(8,128)(2,1)S(1)}, bf16[768,16]{0,1:T(8,128)(2,1)}, u32[]{:S(2)}) copy-start(bf16[768,16]{0,1:T(8,128)(2,1)} %copy-done.31) | copy-start | bytes 73732
  326.7 6.9 %copy-start.21 = (bf16[768,16]{0,1:T(8,128)(2,1)S(1)}, bf16[768,16]{0,1:T(8,128)(2,1)}, u32[]{:S(2)}) copy-start(bf16[768,16]{0,1:T(8,128)(2,1)} %copy-done.20) | copy-start | bytes 73732
  326.7 7.2 %copy-start.25 = (bf16[768,16]{0,1:T(8,128)(2,1)S(1)}, bf16[768,16]{0,1:T(8,128)(2,1)}, u32[]{:S(2)}) copy-start(bf16[768,16]{0,1:T(8,128)(2,1)} %copy-done.24) | copy-start | bytes 73732
  539.9 18.5 %all-to-all-start.1 = ((bf16[96,8,512]{2,0,1:T(8,128)(2,1)}), bf16[96,8,512]{2,0,1:T(8,128)(2,1)S(1)}, u32[]{:S(2)}, u32[]{:S(2)}) async-start(bf16[96,8,512]{2,0,1:T(8,128)(2,1)} %pad_maximum_fusion.1), calls=%async_computation.1 | async-start | bytes 1572864 | tf_op jit(solution)/shard_map/all_to_all | solution.py:178
  (20 other events, 63.6 us)
Sparse Core Ops, SparseCore 0:
  58.9 89.7 all-gather.2
  150.9 89.5 all-gather.4
  286.9 82.4 all-reduce.6
  372.7 81.1 reduce-scatter.6
  457.2 80.4 reduce-scatter.8
where the time goes:
time: 576 us; the launch traced here: 568 us
  waiting for transfers between devices  324 us (56%)
  matrix products  136 us (24%)
  blocking collectives  45.7 us (8%)
  local copies, waits for them, and re-layouts  33 us (6%)
  between operations  15.6 us (3%)
  other arithmetic  6.67 us (1%)
  starting transfers between devices  6.65 us (1%)
    unnamed x8, waiting for transfers between devices  182 us
    dot_general x40, matrix products, contract_pair(): lax.dot_general(left, right, (((left_axis,), (right_axis,)), ((), ())), p...  136 us
    all_gather x2, waiting for transfers between devices, local(): gathered = lax.all_gather(part, 'dp', axis=0, tiled=True)  131 us
    all_to_all x1, blocking collectives, local(): lax.all_to_all(send_both, 'expert', split_axis=0, concat_axis=2, tiled=True)  27.4 us
    all_gather x1, blocking collectives, local(): lax.all_gather(lora_part, 'dp', axis=0, tiled=True).astype(jnp.float32)  18.3 us
  transfers between devices with their start and end apart: 6, of which 6 were waited for; matrix products, arithmetic and copies ran while one was open for 17% of the time, Pallas kernels for 0%

commit v1 on v0

--- a/solution.py
+++ b/solution.py
@@ -149,7 +149,14 @@
     owned_total = None
     for c in range(chunks):
         part = recv_both[c * piece : (c + 1) * piece]
-        gathered = lax.all_gather(part, "dp", axis=0, tiled=True)
+        ring = [part]
+        for hop in range(15):
+            ring.append(lax.ppermute(ring[-1], "dp", [(dev, (dev + 1) % 16) for dev in range(16)]))
+        gathered = jnp.roll(
+            jnp.concatenate(ring[::-1], axis=0),
+            (lax.axis_index("dp") + 1) * ring[0].shape[0],
+            axis=0,
+        )
         x_rows = gathered[:, :complete_width]
         dy_rows = gathered[:, complete_width:]
         rows_out, shared_slice, owned_slice = rows_backward_pass(x_rows, dy_rows, params)

time: 576 us -> 982 us (1.70)
  waiting for transfers between devices: 324 us -> 675 us
  local copies, waits for them, and re-layouts: 33 us -> 69.6 us
  other arithmetic: 6.67 us -> 32.6 us
  matrix products: 136 us -> 124 us
    ppermute x0 -> x30, waiting for transfers between devices: none -> 480 us  [local(): lax.ppermute(ring[-1], 'dp', [(dev, (dev + 1) % 16) for dev in range(16)])]
    all_gather x2 -> x0, waiting for transfers between devices: 131 us -> none  [local(): gathered = lax.all_gather(part, 'dp', axis=0, tiled=True)]
    unnamed x99 -> x175, local copies, waits for them, and re-layouts: 9.66 us -> 43.3 us
    concatenate x0 -> x2, other arithmetic: none -> 26 us  [local(): jnp.roll(jnp.concatenate(ring[::-1], axis=0), (lax.axis_index('dp') + 1)...]
    dot_general x40, matrix products: 136 us -> 124 us  [contract_pair(): lax.dot_general(left, right, (((left_axis,), (right_axis,)), ((), ())), p...]
    unnamed x8 -> x6, waiting for transfers between devices: 182 us -> 183 us
  transfers between devices with their start and end apart: 6 -> 34, of which waited for: 6 -> 33; matrix products, arithmetic and copies ran while one was open for 17% -> 8% of each run, Pallas kernels for 0% -> 0%
where the time goes in v1:
time: 982 us; the launch traced here: 973 us
  waiting for transfers between devices  675 us (69%)
  matrix products  124 us (13%)
  local copies, waits for them, and re-layouts  69.6 us (7%)
  blocking collectives  45.5 us (5%)
  other arithmetic  32.6 us (3%)
  between operations  15.8 us (2%)
    ppermute x30, waiting for transfers between devices, local(): lax.ppermute(ring[-1], 'dp', [(dev, (dev + 1) % 16) for dev in range(16)])  480 us
    unnamed x6, waiting for transfers between devices  183 us
    dot_general x40, matrix products, contract_pair(): lax.dot_general(left, right, (((left_axis,), (right_axis,)), ((), ())), p...  124 us
    unnamed x175, local copies, waits for them, and re-layouts  43.3 us
    all_to_all x1, blocking collectives, local(): lax.all_to_all(send_both, 'expert', split_axis=0, concat_axis=2, tiled=True)  27.4 us
    concatenate x2, other arithmetic, local(): jnp.roll(jnp.concatenate(ring[::-1], axis=0), (lax.axis_index('dp') + 1)...  26 us
  transfers between devices with their start and end apart: 34, of which 33 were waited for; matrix products, arithmetic and copies ran while one was open for 8% of the time, Pallas kernels for 0%

profile of v1, /device:TPU:1, one launch (start us, length us, event | category | flops | bytes accessed | tf_op | source)
XLA Modules:
  0.0 972.6 jit_solution(7104543738540236675)
XLA Ops:
  27.3 27.4 %all_to_all.20 = bf16[8,96,1024]{2,1,0:T(8,128)(2,1)S(1)} all-to-all(bf16[8,96,1024]{2,1,0:T(8,128)(2,1)S(1)} %pad_maximum_fusion), channel_id=1, replica_groups=mesh['dp'=16,'expert'=8] {'expert'}, dimensions={0} | all-to-all | bytes 3145728 | tf_op jit(solution)/shard_map/all_to_all | solution.py:144
  63.0 18.4 %collective-permute-done = bf16[48,8192]{1,0:T(8,128)(2,1)S(1)} collective-permute-done((bf16[48,8192]{1,0:T(8,128)(2,1)S(1)}, bf16[48,8192]{1,0:T(8,128)(2,1)S(1)}, u32[]{:S(2)}, u32[]{:S(2)}) %collective-permute-start) | collective-permute-done | bytes 786464 | tf_op jit(solution)/shard_map/ppermute | solution.py:154
  81.4 16.8 %collective-permute-done.15 = bf16[48,8192]{1,0:T(8,128)(2,1)S(1)} collective-permute-done((bf16[48,8192]{1,0:T(8,128)(2,1)S(1)}, bf16[48,8192]{1,0:T(8,128)(2,1)S(1)}, u32[]{:S(2)}, u32[]{:S(2)}) %collective-permute-start.15) | collective-permute-done | bytes 786464 | tf_op jit(solution)/shard_map/ppermute | solution.py:154
  98.2 16.8 %collective-permute-done.1 = bf16[48,8192]{1,0:T(8,128)(2,1)S(1)} collective-permute-done((bf16[48,8192]{1,0:T(8,128)(2,1)S(1)}, bf16[48,8192]{1,0:T(8,128)(2,1)S(1)}, u32[]{:S(2)}, u32[]{:S(2)}) %collective-permute-start.1) | collective-permute-done | bytes 786464 | tf_op jit(solution)/shard_map/ppermute | solution.py:154
  115.1 16.8 %collective-permute-done.16 = bf16[48,8192]{1,0:T(8,128)(2,1)S(1)} collective-permute-done((bf16[48,8192]{1,0:T(8,128)(2,1)S(1)}, bf16[48,8192]{1,0:T(8,128)(2,1)S(1)}, u32[]{:S(2)}, u32[]{:S(2)}) %collective-permute-start.16) | collective-permute-done | bytes 786464 | tf_op jit(solution)/shard_map/ppermute | solution.py:154
  131.9 16.8 %collective-permute-done.2 = bf16[48,8192]{1,0:T(8,128)(2,1)S(1)} collective-permute-done((bf16[48,8192]{1,0:T(8,128)(2,1)S(1)}, bf16[48,8192]{1,0:T(8,128)(2,1)S(1)}, u32[]{:S(2)}, u32[]{:S(2)}) %collective-permute-start.2) | collective-permute-done | bytes 786464 | tf_op jit(solution)/shard_map/ppermute | solution.py:154
  149.3 16.4 %collective-permute-done.17 = bf16[48,8192]{1,0:T(8,128)(2,1)S(1)} collective-permute-done((bf16[48,8192]{1,0:T(8,128)(2,1)S(1)}, bf16[48,8192]{1,0:T(8,128)(2,1)S(1)}, u32[]{:S(2)}, u32[]{:S(2)}) %collective-permute-start.17) | collective-permute-done | bytes 786464 | tf_op jit(solution)/shard_map/ppermute | solution.py:154
  166.5 16.0 %collective-permute-done.3 = bf16[48,8192]{1,0:T(8,128)(2,1)S(1)} collective-permute-done((bf16[48,8192]{1,0:T(8,128)(2,1)S(1)}, bf16[48,8192]{1,0:T(8,128)(2,1)S(1)}, u32[]{:S(2)}, u32[]{:S(2)}) %collective-permute-start.3) | collective-permute-done | bytes 786464 | tf_op jit(solution)/shard_map/ppermute | solution.py:154
  182.5 16.8 %collective-permute-done.18 = bf16[48,8192]{1,0:T(8,128)(2,1)S(1)} collective-permute-done((bf16[48,8192]{1,0:T(8,128)(2,1)S(1)}, bf16[48,8192]{1,0:T(8,128)(2,1)S(1)}, u32[]{:S(2)}, u32[]{:S(2)}) %collective-permute-start.18) | collective-permute-done | bytes 786464 | tf_op jit(solution)/shard_map/ppermute | solution.py:154
  200.3 16.0 %collective-permute-done.4 = bf16[48,8192]{1,0:T(8,128)(2,1)S(1)} collective-permute-done((bf16[48,8192]{1,0:T(8,128)(2,1)S(1)}, bf16[48,8192]{1,0:T(8,128)(2,1)S(1)}, u32[]{:S(2)}, u32[]{:S(2)}) %collective-permute-start.4) | collective-permute-done | bytes 786464 | tf_op jit(solution)/shard_map/ppermute | solution.py:154
  216.2 16.8 %collective-permute-done.19 = bf16[48,8192]{1,0:T(8,128)(2,1)S(1)} collective-permute-done((bf16[48,8192]{1,0:T(8,128)(2,1)S(1)}, bf16[48,8192]{1,0:T(8,128)(2,1)S(1)}, u32[]{:S(2)}, u32[]{:S(2)}) %collective-permute-start.19) | collective-permute-done | bytes 786464 | tf_op jit(solution)/shard_map/ppermute | solution.py:154
  233.9 16.0 %collective-permute-done.5 = bf16[48,8192]{1,0:T(8,128)(2,1)S(1)} collective-permute-done((bf16[48,8192]{1,0:T(8,128)(2,1)S(1)}, bf16[48,8192]{1,0:T(8,128)(2,1)S(1)}, u32[]{:S(2)}, u32[]{:S(2)}) %collective-permute-start.5) | collective-permute-done | bytes 786464 | tf_op jit(solution)/shard_map/ppermute | solution.py:154
  249.9 16.8 %collective-permute-done.20 = bf16[48,8192]{1,0:T(8,128)(2,1)S(1)} collective-permute-done((bf16[48,8192]{1,0:T(8,128)(2,1)S(1)}, bf16[48,8192]{1,0:T(8,128)(2,1)S(1)}, u32[]{:S(2)}, u32[]{:S(2)}) %collective-permute-start.20) | collective-permute-done | bytes 786464 | tf_op jit(solution)/shard_map/ppermute | solution.py:154
  267.7 15.9 %collective-permute-done.6 = bf16[48,8192]{1,0:T(8,128)(2,1)S(1)} collective-permute-done((bf16[48,8192]{1,0:T(8,128)(2,1)S(1)}, bf16[48,8192]{1,0:T(8,128)(2,1)S(1)}, u32[]{:S(2)}, u32[]{:S(2)}) %collective-permute-start.6) | collective-permute-done | bytes 786464 | tf_op jit(solution)/shard_map/ppermute | solution.py:154
  283.6 16.8 %collective-permute-done.21 = bf16[48,8192]{1,0:T(8,128)(2,1)S(1)} collective-permute-done((bf16[48,8192]{1,0:T(8,128)(2,1)S(1)}, bf16[48,8192]{1,0:T(8,128)(2,1)S(1)}, u32[]{:S(2)}, u32[]{:S(2)}) %collective-permute-start.21) | collective-permute-done | bytes 786464 | tf_op jit(solution)/shard_map/ppermute | solution.py:154
  301.4 15.9 %collective-permute-done.7 = bf16[48,8192]{1,0:T(8,128)(2,1)S(1)} collective-permute-done((bf16[48,8192]{1,0:T(8,128)(2,1)S(1)}, bf16[48,8192]{1,0:T(8,128)(2,1)S(1)}, u32[]{:S(2)}, u32[]{:S(2)}) %collective-permute-start.7) | collective-permute-done | bytes 786464 | tf_op jit(solution)/shard_map/ppermute | solution.py:154
  317.3 16.8 %collective-permute-done.22 = bf16[48,8192]{1,0:T(8,128)(2,1)S(1)} collective-permute-done((bf16[48,8192]{1,0:T(8,128)(2,1)S(1)}, bf16[48,8192]{1,0:T(8,128)(2,1)S(1)}, u32[]{:S(2)}, u32[]{:S(2)}) %collective-permute-start.22) | collective-permute-done | bytes 786464 | tf_op jit(solution)/shard_map/ppermute | solution.py:154
  351.0 16.8 %collective-permute-done.23 = bf16[48,8192]{1,0:T(8,128)(2,1)S(1)} collective-permute-done((bf16[48,8192]{1,0:T(8,128)(2,1)S(1)}, bf16[48,8192]{1,0:T(8,128)(2,1)S(1)}, u32[]{:S(2)}, u32[]{:S(2)}) %collective-permute-start.23) | collective-permute-done | bytes 786464 | tf_op jit(solution)/shard_map/ppermute | solution.py:154
  384.7 16.8 %collective-permute-done.24 = bf16[48,8192]{1,0:T(8,128)(2,1)S(1)} collective-permute-done((bf16[48,8192]{1,0:T(8,128)(2,1)S(1)}, bf16[48,8192]{1,0:T(8,128)(2,1)S(1)}, u32[]{:S(2)}, u32[]{:S(2)}) %collective-permute-start.24) | collective-permute-done | bytes 786464 | tf_op jit(solution)/shard_map/ppermute | solution.py:154
  402.5 16.0 %collective-permute-done.10 = bf16[48,8192]{1,0:T(8,128)(2,1)S(1)} collective-permute-done((bf16[48,8192]{1,0:T(8,128)(2,1)S(1)}, bf16[48,8192]{1,0:T(8,128)(2,1)S(1)}, u32[]{:S(2)}, u32[]{:S(2)}) %collective-permute-start.10) | collective-permute-done | bytes 786464 | tf_op jit(solution)/shard_map/ppermute | solution.py:154
  418.5 16.8 %collective-permute-done.25 = bf16[48,8192]{1,0:T(8,128)(2,1)S(1)} collective-permute-done((bf16[48,8192]{1,0:T(8,128)(2,1)S(1)}, bf16[48,8192]{1,0:T(8,128)(2,1)S(1)}, u32[]{:S(2)}, u32[]{:S(2)}) %collective-permute-start.25) | collective-permute-done | bytes 786464 | tf_op jit(solution)/shard_map/ppermute | solution.py:154
  436.2 15.9 %collective-permute-done.11 = bf16[48,8192]{1,0:T(8,128)(2,1)S(1)} collective-permute-done((bf16[48,8192]{1,0:T(8,128)(2,1)S(1)}, bf16[48,8192]{1,0:T(8,128)(2,1)S(1)}, u32[]{:S(2)}, u32[]{:S(2)}) %collective-permute-start.11) | collective-permute-done | bytes 786464 | tf_op jit(solution)/shard_map/ppermute | solution.py:154
  452.2 16.8 %collective-permute-done.26 = bf16[48,8192]{1,0:T(8,128)(2,1)S(1)} collective-permute-done((bf16[48,8192]{1,0:T(8,128)(2,1)S(1)}, bf16[48,8192]{1,0:T(8,128)(2,1)S(1)}, u32[]{:S(2)}, u32[]{:S(2)}) %collective-permute-start.26) | collective-permute-done | bytes 786464 | tf_op jit(solution)/shard_map/ppermute | solution.py:154
  469.9 16.0 %collective-permute-done.12 = bf16[48,8192]{1,0:T(8,128)(2,1)S(1)} collective-permute-done((bf16[48,8192]{1,0:T(8,128)(2,1)S(1)}, bf16[48,8192]{1,0:T(8,128)(2,1)S(1)}, u32[]{:S(2)}, u32[]{:S(2)}) %collective-permute-start.12) | collective-permute-done | bytes 786464 | tf_op jit(solution)/shard_map/ppermute | solution.py:154
  485.9 17.0 %collective-permute-done.27 = bf16[48,8192]{1,0:T(8,128)(2,1)} collective-permute-done((bf16[48,8192]{1,0:T(8,128)(2,1)S(1)}, bf16[48,8192]{1,0:T(8,128)(2,1)}, u32[]{:S(2)}, u32[]{:S(2)}) %collective-permute-start.27) | collective-permute-done | bytes 786464 | tf_op jit(solution)/shard_map/ppermute | solution.py:154
  502.8 16.8 %collective-permute-done.13 = bf16[48,8192]{1,0:T(8,128)(2,1)} collective-permute-done((bf16[48,8192]{1,0:T(8,128)(2,1)S(1)}, bf16[48,8192]{1,0:T(8,128)(2,1)}, u32[]{:S(2)}, u32[]{:S(2)}) %collective-permute-start.13) | collective-permute-done | bytes 786464 | tf_op jit(solution)/shard_map/ppermute | solution.py:154
  519.8 16.7 %collective-permute-done.28 = bf16[48,8192]{1,0:T(8,128)(2,1)} collective-permute-done((bf16[48,8192]{1,0:T(8,128)(2,1)}, bf16[48,8192]{1,0:T(8,128)(2,1)}, u32[]{:S(2)}, u32[]{:S(2)}) %collective-permute-start.28) | collective-permute-done | bytes 786464 | tf_op jit(solution)/shard_map/ppermute | solution.py:154
  536.7 16.7 %collective-permute-done.14 = bf16[48,8192]{1,0:T(8,128)(2,1)} collective-permute-done((bf16[48,8192]{1,0:T(8,128)(2,1)}, bf16[48,8192]{1,0:T(8,128)(2,1)}, u32[]{:S(2)}, u32[]{:S(2)}) %collective-permute-start.14) | collective-permute-done | bytes 786464 | tf_op jit(solution)/shard_map/ppermute | solution.py:154
  738.2 35.0 %all-reduce.7.cloned.1.call-done = bf16[128,1536]{1,0:T(8,128)(2,1)} async-done(((bf16[128,1536]{1,0:T(8,128)(2,1)}), bf16[128,1536]{1,0:T(8,128)(2,1)}) %all-reduce.7.cloned.1.call-update) | async-done | bytes 393232
  773.9 18.1 %all_gather.3 = bf16[128,1536]{1,0:T(8,128)(2,1)S(1)} all-gather(bf16[8,1536]{1,0:T(8,128)(2,1)S(1)} %constant_dynamic-slice_fusion), channel_id=1, replica_groups=mesh['dp'=16,'expert'=8] {'dp'}, dimensions={0}, use_global_device_ids=true | all-gather | bytes 417792 | tf_op jit(solution)/shard_map/all_gather | solution.py:180
  792.4 65.5 %reduce-scatter.7.cloned.1.call-done = bf16[1,48,4096]{2,1,0:T(8,128)(2,1)} async-done(((bf16[16,48,4096]{2,1,0:T(8,128)(2,1)}), bf16[1,48,4096]{2,1,0:T(8,128)(2,1)}) %reduce-scatter.7.cloned.1.call-update) | async-done | bytes 393232
  859.1 82.8 %reduce-scatter.9.cloned.1.call-done = bf16[1,48,4096]{2,1,0:T(8,128)(2,1)} async-done(((bf16[16,48,4096]{2,1,0:T(8,128)(2,1)}), bf16[1,48,4096]{2,1,0:T(8,128)(2,1)}) %reduce-scatter.9.cloned.1.call-update) | async-done | bytes 393232
  (307 shorter events, 279.4 us)
Async XLA Ops:
  7.2 765.9 %all-reduce.7.cloned.1.call-start = ((), (), s32[]{:S(2)}) async-start(), calls=%async_computation.4 | async-start | bytes 786432
  61.6 36.6 %collective-permute-start.15 = (bf16[48,8192]{1,0:T(8,128)(2,1)S(1)}, bf16[48,8192]{1,0:T(8,128)(2,1)S(1)}, u32[]{:S(2)}, u32[]{:S(2)}) collective-permute-start(bf16[48,8192]{1,0:T(8,128)(2,1)S(1)} %bitcast.247), channel_id=1, source_target_pairs={{0,8},{8,16},{16,24},{24,32},{32,40},{40,48},{48,56},{56,64},{64,7... | collective-permute-start | bytes 2359304 | tf_op jit(solution)/shard_map/ppermute | solution.py:154
  81.4 33.7 %collective-permute-start.1 = (bf16[48,8192]{1,0:T(8,128)(2,1)S(1)}, bf16[48,8192]{1,0:T(8,128)(2,1)S(1)}, u32[]{:S(2)}, u32[]{:S(2)}) collective-permute-start(bf16[48,8192]{1,0:T(8,128)(2,1)S(1)} %collective-permute-done), channel_id=1, source_target_pairs={{0,8},{8,16},{16,24},{24,32},{32,40},{40,48},{48,56},{56,64},{64,7... | collective-permute-start | bytes 2359304 | tf_op jit(solution)/shard_map/ppermute | solution.py:154
  98.2 33.7 %collective-permute-start.16 = (bf16[48,8192]{1,0:T(8,128)(2,1)S(1)}, bf16[48,8192]{1,0:T(8,128)(2,1)S(1)}, u32[]{:S(2)}, u32[]{:S(2)}) collective-permute-start(bf16[48,8192]{1,0:T(8,128)(2,1)S(1)} %collective-permute-done.15), channel_id=1, source_target_pairs={{0,8},{8,16},{16,24},{24,32},{32,40},{40,48},{48,56},{56,64},{64,7... | collective-permute-start | bytes 2359304 | tf_op jit(solution)/shard_map/ppermute | solution.py:154
  115.1 33.7 %collective-permute-start.2 = (bf16[48,8192]{1,0:T(8,128)(2,1)S(1)}, bf16[48,8192]{1,0:T(8,128)(2,1)S(1)}, u32[]{:S(2)}, u32[]{:S(2)}) collective-permute-start(bf16[48,8192]{1,0:T(8,128)(2,1)S(1)} %collective-permute-done.1), channel_id=1, source_target_pairs={{0,8},{8,16},{16,24},{24,32},{32,40},{40,48},{48,56},{56,64},{64,7... | collective-permute-start | bytes 2359304 | tf_op jit(solution)/shard_map/ppermute | solution.py:154
  131.9 33.7 %collective-permute-start.17 = (bf16[48,8192]{1,0:T(8,128)(2,1)S(1)}, bf16[48,8192]{1,0:T(8,128)(2,1)S(1)}, u32[]{:S(2)}, u32[]{:S(2)}) collective-permute-start(bf16[48,8192]{1,0:T(8,128)(2,1)S(1)} %collective-permute-done.16), channel_id=1, source_target_pairs={{0,8},{8,16},{16,24},{24,32},{32,40},{40,48},{48,56},{56,64},{64,7... | collective-permute-start | bytes 2359304 | tf_op jit(solution)/shard_map/ppermute | solution.py:154
  148.8 33.7 %collective-permute-start.3 = (bf16[48,8192]{1,0:T(8,128)(2,1)S(1)}, bf16[48,8192]{1,0:T(8,128)(2,1)S(1)}, u32[]{:S(2)}, u32[]{:S(2)}) collective-permute-start(bf16[48,8192]{1,0:T(8,128)(2,1)S(1)} %collective-permute-done.2), channel_id=1, source_target_pairs={{0,8},{8,16},{16,24},{24,32},{32,40},{40,48},{48,56},{56,64},{64,7... | collective-permute-start | bytes 2359304 | tf_op jit(solution)/shard_map/ppermute | solution.py:154
  166.5 32.8 %collective-permute-start.18 = (bf16[48,8192]{1,0:T(8,128)(2,1)S(1)}, bf16[48,8192]{1,0:T(8,128)(2,1)S(1)}, u32[]{:S(2)}, u32[]{:S(2)}) collective-permute-start(bf16[48,8192]{1,0:T(8,128)(2,1)S(1)} %collective-permute-done.17), channel_id=1, source_target_pairs={{0,8},{8,16},{16,24},{24,32},{32,40},{40,48},{48,56},{56,64},{64,7... | collective-permute-start | bytes 2359304 | tf_op jit(solution)/shard_map/ppermute | solution.py:154
  182.5 33.7 %collective-permute-start.4 = (bf16[48,8192]{1,0:T(8,128)(2,1)S(1)}, bf16[48,8192]{1,0:T(8,128)(2,1)S(1)}, u32[]{:S(2)}, u32[]{:S(2)}) collective-permute-start(bf16[48,8192]{1,0:T(8,128)(2,1)S(1)} %collective-permute-done.3), channel_id=1, source_target_pairs={{0,8},{8,16},{16,24},{24,32},{32,40},{40,48},{48,56},{56,64},{64,7... | collective-permute-start | bytes 2359304 | tf_op jit(solution)/shard_map/ppermute | solution.py:154
  199.4 33.7 %collective-permute-start.19 = (bf16[48,8192]{1,0:T(8,128)(2,1)S(1)}, bf16[48,8192]{1,0:T(8,128)(2,1)S(1)}, u32[]{:S(2)}, u32[]{:S(2)}) collective-permute-start(bf16[48,8192]{1,0:T(8,128)(2,1)S(1)} %collective-permute-done.18), channel_id=1, source_target_pairs={{0,8},{8,16},{16,24},{24,32},{32,40},{40,48},{48,56},{56,64},{64,7... | collective-permute-start | bytes 2359304 | tf_op jit(solution)/shard_map/ppermute | solution.py:154
  216.2 33.7 %collective-permute-start.5 = (bf16[48,8192]{1,0:T(8,128)(2,1)S(1)}, bf16[48,8192]{1,0:T(8,128)(2,1)S(1)}, u32[]{:S(2)}, u32[]{:S(2)}) collective-permute-start(bf16[48,8192]{1,0:T(8,128)(2,1)S(1)} %collective-permute-done.4), channel_id=1, source_target_pairs={{0,8},{8,16},{16,24},{24,32},{32,40},{40,48},{48,56},{56,64},{64,7... | collective-permute-start | bytes 2359304 | tf_op jit(solution)/shard_map/ppermute | solution.py:154
  233.9 32.8 %collective-permute-start.20 = (bf16[48,8192]{1,0:T(8,128)(2,1)S(1)}, bf16[48,8192]{1,0:T(8,128)(2,1)S(1)}, u32[]{:S(2)}, u32[]{:S(2)}) collective-permute-start(bf16[48,8192]{1,0:T(8,128)(2,1)S(1)} %collective-permute-done.19), channel_id=1, source_target_pairs={{0,8},{8,16},{16,24},{24,32},{32,40},{40,48},{48,56},{56,64},{64,7... | collective-permute-start | bytes 2359304 | tf_op jit(solution)/shard_map/ppermute | solution.py:154
  249.9 33.7 %collective-permute-start.6 = (bf16[48,8192]{1,0:T(8,128)(2,1)S(1)}, bf16[48,8192]{1,0:T(8,128)(2,1)S(1)}, u32[]{:S(2)}, u32[]{:S(2)}) collective-permute-start(bf16[48,8192]{1,0:T(8,128)(2,1)S(1)} %collective-permute-done.5), channel_id=1, source_target_pairs={{0,8},{8,16},{16,24},{24,32},{32,40},{40,48},{48,56},{56,64},{64,7... | collective-permute-start | bytes 2359304 | tf_op jit(solution)/shard_map/ppermute | solution.py:154
  266.8 33.7 %collective-permute-start.21 = (bf16[48,8192]{1,0:T(8,128)(2,1)S(1)}, bf16[48,8192]{1,0:T(8,128)(2,1)S(1)}, u32[]{:S(2)}, u32[]{:S(2)}) collective-permute-start(bf16[48,8192]{1,0:T(8,128)(2,1)S(1)} %collective-permute-done.20), channel_id=1, source_target_pairs={{0,8},{8,16},{16,24},{24,32},{32,40},{40,48},{48,56},{56,64},{64,7... | collective-permute-start | bytes 2359304 | tf_op jit(solution)/shard_map/ppermute | solution.py:154
  283.6 33.7 %collective-permute-start.7 = (bf16[48,8192]{1,0:T(8,128)(2,1)S(1)}, bf16[48,8192]{1,0:T(8,128)(2,1)S(1)}, u32[]{:S(2)}, u32[]{:S(2)}) collective-permute-start(bf16[48,8192]{1,0:T(8,128)(2,1)S(1)} %collective-permute-done.6), channel_id=1, source_target_pairs={{0,8},{8,16},{16,24},{24,32},{32,40},{40,48},{48,56},{56,64},{64,7... | collective-permute-start | bytes 2359304 | tf_op jit(solution)/shard_map/ppermute | solution.py:154
  300.5 33.7 %collective-permute-start.22 = (bf16[48,8192]{1,0:T(8,128)(2,1)S(1)}, bf16[48,8192]{1,0:T(8,128)(2,1)S(1)}, u32[]{:S(2)}, u32[]{:S(2)}) collective-permute-start(bf16[48,8192]{1,0:T(8,128)(2,1)S(1)} %collective-permute-done.21), channel_id=1, source_target_pairs={{0,8},{8,16},{16,24},{24,32},{32,40},{40,48},{48,56},{56,64},{64,7... | collective-permute-start | bytes 2359304 | tf_op jit(solution)/shard_map/ppermute | solution.py:154
  317.3 33.7 %collective-permute-start.8 = (bf16[48,8192]{1,0:T(8,128)(2,1)S(1)}, bf16[48,8192]{1,0:T(8,128)(2,1)S(1)}, u32[]{:S(2)}, u32[]{:S(2)}) collective-permute-start(bf16[48,8192]{1,0:T(8,128)(2,1)S(1)} %collective-permute-done.7), channel_id=1, source_target_pairs={{0,8},{8,16},{16,24},{24,32},{32,40},{40,48},{48,56},{56,64},{64,7... | collective-permute-start | bytes 2359304 | tf_op jit(solution)/shard_map/ppermute | solution.py:154
  334.2 33.7 %collective-permute-start.23 = (bf16[48,8192]{1,0:T(8,128)(2,1)S(1)}, bf16[48,8192]{1,0:T(8,128)(2,1)S(1)}, u32[]{:S(2)}, u32[]{:S(2)}) collective-permute-start(bf16[48,8192]{1,0:T(8,128)(2,1)S(1)} %collective-permute-done.22), channel_id=1, source_target_pairs={{0,8},{8,16},{16,24},{24,32},{32,40},{40,48},{48,56},{56,64},{64,7... | collective-permute-start | bytes 2359304 | tf_op jit(solution)/shard_map/ppermute | solution.py:154
  351.0 33.7 %collective-permute-start.9 = (bf16[48,8192]{1,0:T(8,128)(2,1)S(1)}, bf16[48,8192]{1,0:T(8,128)(2,1)S(1)}, u32[]{:S(2)}, u32[]{:S(2)}) collective-permute-start(bf16[48,8192]{1,0:T(8,128)(2,1)S(1)} %collective-permute-done.8), channel_id=1, source_target_pairs={{0,8},{8,16},{16,24},{24,32},{32,40},{40,48},{48,56},{56,64},{64,7... | collective-permute-start | bytes 2359304 | tf_op jit(solution)/shard_map/ppermute | solution.py:154
  367.9 33.7 %collective-permute-start.24 = (bf16[48,8192]{1,0:T(8,128)(2,1)S(1)}, bf16[48,8192]{1,0:T(8,128)(2,1)S(1)}, u32[]{:S(2)}, u32[]{:S(2)}) collective-permute-start(bf16[48,8192]{1,0:T(8,128)(2,1)S(1)} %collective-permute-done.23), channel_id=1, source_target_pairs={{0,8},{8,16},{16,24},{24,32},{32,40},{40,48},{48,56},{56,64},{64,7... | collective-permute-start | bytes 2359304 | tf_op jit(solution)/shard_map/ppermute | solution.py:154
  384.7 33.7 %collective-permute-start.10 = (bf16[48,8192]{1,0:T(8,128)(2,1)S(1)}, bf16[48,8192]{1,0:T(8,128)(2,1)S(1)}, u32[]{:S(2)}, u32[]{:S(2)}) collective-permute-start(bf16[48,8192]{1,0:T(8,128)(2,1)S(1)} %collective-permute-done.9), channel_id=1, source_target_pairs={{0,8},{8,16},{16,24},{24,32},{32,40},{40,48},{48,56},{56,64},{64,7... | collective-permute-start | bytes 2359304 | tf_op jit(solution)/shard_map/ppermute | solution.py:154
  401.6 33.7 %collective-permute-start.25 = (bf16[48,8192]{1,0:T(8,128)(2,1)S(1)}, bf16[48,8192]{1,0:T(8,128)(2,1)S(1)}, u32[]{:S(2)}, u32[]{:S(2)}) collective-permute-start(bf16[48,8192]{1,0:T(8,128)(2,1)S(1)} %collective-permute-done.24), channel_id=1, source_target_pairs={{0,8},{8,16},{16,24},{24,32},{32,40},{40,48},{48,56},{56,64},{64,7... | collective-permute-start | bytes 2359304 | tf_op jit(solution)/shard_map/ppermute | solution.py:154
  418.4 33.7 %collective-permute-start.11 = (bf16[48,8192]{1,0:T(8,128)(2,1)S(1)}, bf16[48,8192]{1,0:T(8,128)(2,1)S(1)}, u32[]{:S(2)}, u32[]{:S(2)}) collective-permute-start(bf16[48,8192]{1,0:T(8,128)(2,1)S(1)} %collective-permute-done.10), channel_id=1, source_target_pairs={{0,8},{8,16},{16,24},{24,32},{32,40},{40,48},{48,56},{56,64},{64,7... | collective-permute-start | bytes 2359304 | tf_op jit(solution)/shard_map/ppermute | solution.py:154
  435.3 33.7 %collective-permute-start.26 = (bf16[48,8192]{1,0:T(8,128)(2,1)S(1)}, bf16[48,8192]{1,0:T(8,128)(2,1)S(1)}, u32[]{:S(2)}, u32[]{:S(2)}) collective-permute-start(bf16[48,8192]{1,0:T(8,128)(2,1)S(1)} %collective-permute-done.25), channel_id=1, source_target_pairs={{0,8},{8,16},{16,24},{24,32},{32,40},{40,48},{48,56},{56,64},{64,7... | collective-permute-start | bytes 2359304 | tf_op jit(solution)/shard_map/ppermute | solution.py:154
  452.2 33.7 %collective-permute-start.12 = (bf16[48,8192]{1,0:T(8,128)(2,1)S(1)}, bf16[48,8192]{1,0:T(8,128)(2,1)S(1)}, u32[]{:S(2)}, u32[]{:S(2)}) collective-permute-start(bf16[48,8192]{1,0:T(8,128)(2,1)S(1)} %collective-permute-done.11), channel_id=1, source_target_pairs={{0,8},{8,16},{16,24},{24,32},{32,40},{40,48},{48,56},{56,64},{64,7... | collective-permute-start | bytes 2359304 | tf_op jit(solution)/shard_map/ppermute | solution.py:154
  469.0 33.8 %collective-permute-start.27 = (bf16[48,8192]{1,0:T(8,128)(2,1)S(1)}, bf16[48,8192]{1,0:T(8,128)(2,1)}, u32[]{:S(2)}, u32[]{:S(2)}) collective-permute-start(bf16[48,8192]{1,0:T(8,128)(2,1)S(1)} %collective-permute-done.26), channel_id=1, source_target_pairs={{0,8},{8,16},{16,24},{24,32},{32,40},{40,48},{48,56},{56,64},{64,7... | collective-permute-start | bytes 2359304 | tf_op jit(solution)/shard_map/ppermute | solution.py:154
  485.9 33.8 %collective-permute-start.13 = (bf16[48,8192]{1,0:T(8,128)(2,1)S(1)}, bf16[48,8192]{1,0:T(8,128)(2,1)}, u32[]{:S(2)}, u32[]{:S(2)}) collective-permute-start(bf16[48,8192]{1,0:T(8,128)(2,1)S(1)} %collective-permute-done.12), channel_id=1, source_target_pairs={{0,8},{8,16},{16,24},{24,32},{32,40},{40,48},{48,56},{56,64},{64,7... | collective-permute-start | bytes 2359304 | tf_op jit(solution)/shard_map/ppermute | solution.py:154
  502.8 33.7 %collective-permute-start.28 = (bf16[48,8192]{1,0:T(8,128)(2,1)}, bf16[48,8192]{1,0:T(8,128)(2,1)}, u32[]{:S(2)}, u32[]{:S(2)}) collective-permute-start(bf16[48,8192]{1,0:T(8,128)(2,1)} %collective-permute-done.27), channel_id=1, source_target_pairs={{0,8},{8,16},{16,24},{24,32},{32,40},{40,48},{48,56},{56,64},{64,7... | collective-permute-start | bytes 2359304 | tf_op jit(solution)/shard_map/ppermute | solution.py:154
  519.7 33.7 %collective-permute-start.14 = (bf16[48,8192]{1,0:T(8,128)(2,1)}, bf16[48,8192]{1,0:T(8,128)(2,1)}, u32[]{:S(2)}, u32[]{:S(2)}) collective-permute-start(bf16[48,8192]{1,0:T(8,128)(2,1)} %collective-permute-done.13), channel_id=1, source_target_pairs={{0,8},{8,16},{16,24},{24,32},{32,40},{40,48},{48,56},{56,64},{64,7... | collective-permute-start | bytes 2359304 | tf_op jit(solution)/shard_map/ppermute | solution.py:154
  536.5 43.3 %collective-permute-start.29 = (bf16[48,8192]{1,0:T(8,128)(2,1)}, bf16[48,8192]{1,0:T(8,128)(2,1)S(1)}, u32[]{:S(2)}, u32[]{:S(2)}) collective-permute-start(bf16[48,8192]{1,0:T(8,128)(2,1)} %collective-permute-done.28), channel_id=1, source_target_pairs={{0,8},{8,16},{16,24},{24,32},{32,40},{40,48},{48,56},{56,64},{64,7... | collective-permute-start | bytes 2359304 | tf_op jit(solution)/shard_map/ppermute | solution.py:154
  691.4 166.5 %reduce-scatter.7.cloned.1.call-start = ((), (), s32[]{:S(2)}) async-start(), calls=%async_computation.5 | async-start | bytes 6684672
  703.5 238.4 %reduce-scatter.9.cloned.1.call-start = ((), (), s32[]{:S(2)}) async-start(), calls=%async_computation.6 | async-start | bytes 6684672
  (71 other events, 3109.1 us)
Sparse Core Ops, SparseCore 0:
  691.5 81.5 all-reduce.6
  776.5 81.3 reduce-scatter.6
  861.3 80.5 reduce-scatter.8
